TPU v7x, 512 devices: a whole 4x4x16 slice. The times are simulated.
512 devices in a mesh: dp: 16 (over x, z_lo), expert: 32 (over y, z_hi, core).
Axes of the slice: x: 4, y: 4, z: 16 (z_hi: 4, z_lo: 4; z = z_hi * 4 + z_lo), core: 2. Of those that a mesh axis runs over, the one named last changes fastest.
Arguments:
- tokens: bfloat16 [4096, 2560], P(('dp', 'expert')), may hold values from -24 to 24
- routes: int32 [4096, 6], P(('dp', 'expert')), may hold values from 0 to 7, all different within a row; in each aligned block of 8 rows (0 to 7, 8 to 15, ...) at most 7 rows name the same one
- router: float32 [2560, 8], replicated, may hold values from -0.125 to 0.125
- w_gate: bfloat16 [2560, 8192], P(None, 'expert'), may hold values from -0.125 to 0.125
- w_up: bfloat16 [2560, 8192], P(None, 'expert'), may hold values from -0.125 to 0.125
- w_down: bfloat16 [2560, 8192], P(None, 'expert'), may hold values from -0.1875 to 0.1875
- cotangent: bfloat16 [4096, 2560], P(('dp', 'expert')), may hold values from -6 to 6
Outputs:
- mixed: bfloat16 [4096, 2560], P(('dp', 'expert'))
- grad_tokens: bfloat16 [4096, 2560], P(('dp', 'expert'))
- grad_router: float32 [2560, 8], replicated
- grad_gate: float32 [2560, 8192], P('dp', 'expert')
- grad_up: float32 [2560, 8192], P('dp', 'expert')
- grad_down: float32 [2560, 8192], P('dp', 'expert')
Inputs may be any that keep to these rules, and one draw needn't show every extreme that they name: `routes`: each row names 6 different experts. Among the rows of one device no expert is named more than 7 times, and in every draw some expert is named exactly 7 times by the rows of some device.
All inputs are finite; a program needn't handle non-finite values.
Results may differ from a plain program's by a relative error of at most 0.02.
Values may be sent and summed in bfloat16 or wider, within the bound.
A program may use at most 64 MiB of HBM per device.

v0:
```python
import jax
import jax.numpy as jnp
from jax import lax
from jax.sharding import PartitionSpec as P


def expert_hidden(inputs, gate_matrix, up_matrix):
    gate_pre = jnp.dot(inputs, gate_matrix, preferred_element_type=jnp.float32)
    up_pre = jnp.dot(inputs, up_matrix, preferred_element_type=jnp.float32)
    hidden = (jax.nn.silu(gate_pre) * up_pre).astype(jnp.bfloat16)
    return (gate_pre, up_pre, hidden)


def expert_backward(slot_grad, gate_pre, up_pre, gate_matrix, up_matrix, down_matrix):
    hidden_grad = jnp.dot(slot_grad, down_matrix, preferred_element_type=jnp.float32)
    sigma = jax.nn.sigmoid(gate_pre)
    gate_grad = (hidden_grad * up_pre * sigma * (1.0 + gate_pre * (1.0 - sigma))).astype(
        jnp.bfloat16
    )
    up_grad = (hidden_grad * gate_pre * sigma).astype(jnp.bfloat16)
    contract = (((1,), (1,)), ((), ()))
    input_grad = lax.dot_general(
        gate_grad, gate_matrix, contract, preferred_element_type=jnp.float32
    )
    input_grad = input_grad + lax.dot_general(
        up_grad, up_matrix, contract, preferred_element_type=jnp.float32
    )
    return (gate_grad, up_grad, input_grad.astype(jnp.bfloat16))


def return_grads(input_part):
    return lax.all_to_all(input_part, "expert", split_axis=0, concat_axis=0, tiled=True)


def local(tokens, routes, router, w_gate, w_up, w_down, cotangent):
    features = tokens.shape[1]
    experts = router.shape[1]
    fanout = routes.shape[1]
    tok_count = tokens.shape[0]
    hidden_units = w_gate.shape[1]
    sharing = lax.axis_size("expert") // experts
    capacity = min(tok_count, 5 * fanout * tok_count // (4 * experts))
    highest = lax.Precision.HIGHEST
    tokens_wide = tokens.astype(jnp.float32)
    logits = jnp.dot(tokens_wide, router, precision=highest)
    expert_ids = jnp.arange(experts, dtype=jnp.int32)
    choose = routes[:, :, None] == expert_ids[None, None, :]
    choose_f = choose.astype(jnp.float32)
    picked = jnp.sum(choose_f * logits[:, None, :], axis=2)
    affinity = jax.nn.sigmoid(picked)
    denominator = jnp.sum(affinity, axis=1, keepdims=True)
    gate_values = affinity / denominator
    choose_i = choose.astype(jnp.int32)
    per_token = jnp.sum(choose_i, axis=1)
    before = jnp.cumsum(per_token, axis=0) - per_token
    position = jnp.sum(choose_i * before[:, None, :], axis=2)
    slot_ids = jnp.arange(capacity, dtype=jnp.int32)
    placed = choose_f[:, :, :, None] * (
        position[:, :, None, None] == slot_ids[None, None, None, :]
    ).astype(jnp.float32)
    slot_table = jnp.sum(placed, axis=1)
    gate_table = jnp.einsum("tkec,tk->tec", placed, gate_values)
    table_narrow = slot_table.astype(jnp.bfloat16)
    outgoing = jnp.einsum(
        "tec,td->ecd", table_narrow, tokens, preferred_element_type=jnp.float32
    ).astype(jnp.bfloat16)
    outgoing_all = jnp.repeat(outgoing, sharing, axis=0)

    def merge_parts(parts):
        wide_parts = parts.astype(jnp.float32)
        return jnp.sum(wide_parts.reshape(experts, sharing, capacity, features), axis=1)

    received = lax.all_to_all(outgoing_all, "expert", split_axis=0, concat_axis=0, tiled=True)
    sources, item_count, _ = received.shape
    expert_rows = received.reshape(sources * item_count, features)
    gate_pre, up_pre, hidden = expert_hidden(expert_rows, w_gate, w_up)
    output = lax.dot_general(
        hidden, w_down, (((1,), (1,)), ((), ())), preferred_element_type=jnp.float32
    )
    output = output.astype(jnp.bfloat16).reshape(sources, item_count, features)
    returned = lax.all_to_all(output, "expert", split_axis=0, concat_axis=0, tiled=True)
    returned, rows_kept, gate_kept, up_kept, hidden_kept = (
        returned,
        received,
        gate_pre.reshape(sources, item_count, hidden_units),
        up_pre.reshape(sources, item_count, hidden_units),
        hidden.reshape(sources, item_count, hidden_units),
    )
    expert_out = merge_parts(returned).astype(jnp.bfloat16)
    expert_wide = lax.optimization_barrier(expert_out).astype(jnp.float32)
    mixed = jnp.einsum("tec,ecd->td", gate_table, expert_wide).astype(jnp.bfloat16)
    grad_slots = jnp.einsum(
        "tec,td->ecd", table_narrow, cotangent, preferred_element_type=jnp.float32
    ).astype(jnp.bfloat16)
    slot_pull = jnp.sum(grad_slots.astype(jnp.float32) * expert_wide, axis=2)
    expert_pull = jnp.einsum("tec,ec->te", slot_table, slot_pull)
    gate_pull = jnp.sum(choose_f * expert_pull[:, None, :], axis=2)
    mean_pull = jnp.sum(gate_values * gate_pull, axis=1, keepdims=True)
    logit_grad = (gate_pull - mean_pull) / denominator * affinity * (1.0 - affinity)
    per_logit = jnp.sum(choose_f * logit_grad[:, :, None], axis=1)
    router_part = jnp.dot(tokens_wide.T, per_logit, precision=highest)
    grad_router = lax.psum(router_part, ("dp", "expert"))
    slot_gate = jnp.sum(gate_table, axis=0)
    grad_outgoing = (slot_gate[:, :, None] * grad_slots.astype(jnp.float32)).astype(jnp.bfloat16)
    grad_outgoing_all = jnp.repeat(grad_outgoing, sharing, axis=0)
    row_items = lax.all_to_all(outgoing_all, "expert", split_axis=0, concat_axis=0, tiled=True)
    grad_items = lax.all_to_all(
        grad_outgoing_all, "expert", split_axis=0, concat_axis=0, tiled=True
    )
    sources, item_count, _ = row_items.shape
    expert_rows = row_items.reshape(-1, features)
    grad_rows = grad_items.reshape(-1, features)
    gate_pre, up_pre, hidden = expert_hidden(expert_rows, w_gate, w_up)
    backward_gate_grad, backward_up_grad, input_part = expert_backward(
        grad_rows, gate_pre, up_pre, w_gate, w_up, w_down
    )
    input_back = return_grads(input_part.reshape(sources, item_count, features))
    input_back, rows_again, grads_again, hidden_again, gate_again, up_again = (
        input_back,
        row_items,
        grad_items,
        hidden.reshape(sources, item_count, hidden_units),
        backward_gate_grad.reshape(sources, item_count, hidden_units),
        backward_up_grad.reshape(sources, item_count, hidden_units),
    )
    rows_flat = rows_again.reshape(-1, features)
    grad_flat = grads_again.reshape(-1, features)
    hidden_flat = hidden_again.reshape(-1, hidden_units)
    gate_grad = gate_again.reshape(-1, hidden_units)
    up_grad = up_again.reshape(-1, hidden_units)
    contract = (((0,), (0,)), ((), ()))
    part_gate = lax.dot_general(rows_flat, gate_grad, contract, preferred_element_type=jnp.float32)
    part_up = lax.dot_general(rows_flat, up_grad, contract, preferred_element_type=jnp.float32)
    part_down = lax.dot_general(
        grad_flat, hidden_flat, contract, preferred_element_type=jnp.float32
    )
    summed = lax.psum_scatter(
        jnp.concatenate([part_gate, part_up, part_down], axis=1).astype(jnp.bfloat16),
        "dp",
        scatter_dimension=0,
        tiled=True,
    ).astype(jnp.float32)
    grad_gate = summed[:, :hidden_units]
    grad_up = summed[:, hidden_units : 2 * hidden_units]
    grad_down = summed[:, 2 * hidden_units :]
    input_grad = merge_parts(input_back).astype(jnp.bfloat16)
    input_wide = lax.optimization_barrier(input_grad).astype(jnp.float32)
    router_back = lax.dot_general(per_logit, router, (((1,), (1,)), ((), ())), precision=highest)
    grad_tokens = (jnp.einsum("tec,ecd->td", slot_table, input_wide) + router_back).astype(
        jnp.bfloat16
    )
    return (mixed, grad_tokens, grad_router, grad_gate, grad_up, grad_down)


def solution(mesh):
    return jax.shard_map(
        local,
        mesh=mesh,
        in_specs=(
            P(("dp", "expert"), None),
            P(("dp", "expert"), None),
            P(),
            P(None, "expert"),
            P(None, "expert"),
            P(None, "expert"),
            P(("dp", "expert"), None),
        ),
        out_specs=(
            P(("dp", "expert"), None),
            P(("dp", "expert"), None),
            P(),
            P("dp", "expert"),
            P("dp", "expert"),
            P("dp", "expert"),
        ),
        check_vma=False,
    )
```

profile of v0, /device:TPU:1, one launch (start us, length us, event | category | flops | bytes accessed | tf_op | source)
XLA Modules:
  0.0 811.4 jit_solution(12839090901430853241)
XLA Ops:
  8.0 0.9 copy.37
  9.1 0.2 select_reduce_fusion.3
  9.5 1.0 convolution_convert_fusion.5
  10.7 82.5 %all_to_all.21 = bf16[32,7,2560]{2,1,0:T(8,128)(2,1)} all-to-all(bf16[32,7,2560]{2,1,0:T(8,128)(2,1)S(1)} %bitcast.58), channel_id=1, replica_groups=mesh['dp'=16,'expert'=32] {'expert'}, dimensions={0} | all-to-all | bytes 2293760 | tf_op jit(solution)/shard_map/all_to_all | solution.py:73
  93.2 1.5 reshape.115
  94.7 1.9 fusion.22
  96.6 1.2 multiply_convert_fusion.3
  97.8 1.6 convolution_convert_fusion.3
  99.4 2.3 reshape.116
  101.7 8.7 %all-to-all-start.1 = ((bf16[32,7,2560]{2,1,0:T(8,128)(2,1)}), bf16[32,7,2560]{2,1,0:T(8,128)(2,1)}, u32[]{:S(2)}, u32[]{:S(2)}) async-start(bf16[32,7,2560]{2,1,0:T(8,128)(2,1)} %reshape.116), calls=%async_computation.1 | async-start | bytes 2621440 | tf_op jit(solution)/shard_map/all_to_all | solution.py:81
  110.4 0.8 fusion.21
  111.2 0.7 broadcast_multiply_fusion
  112.0 36.9 %all-to-all-done.1 = bf16[32,7,2560]{2,1,0:T(8,128)(2,1)} async-done(((bf16[32,7,2560]{2,1,0:T(8,128)(2,1)}), bf16[32,7,2560]{2,1,0:T(8,128)(2,1)}, u32[]{:S(2)}, u32[]{:S(2)}) %all-to-all-start.1) | async-done | bytes 1146912 | tf_op jit(solution)/shard_map/all_to_all | solution.py:81
  148.9 1.6 bitcast_reduce_fusion.1
  150.5 1.1 multiply_reduce_fusion
  151.6 0.2 select_reduce_fusion.1
  151.8 0.5 copy-done.13
  152.4 0.6 fusion.19
  152.9 1.4 copy.51
  154.3 1.0 fusion.6
  155.4 0.6 copy-done.10
  156.3 74.3 %all_to_all.22 = bf16[32,7,2560]{2,1,0:T(8,128)(2,1)} all-to-all(bf16[32,7,2560]{2,1,0:T(8,128)(2,1)S(1)} %bitcast.59), channel_id=1, replica_groups=mesh['dp'=16,'expert'=32] {'expert'}, dimensions={0} | all-to-all | bytes 2293760 | tf_op jit(solution)/shard_map/all_to_all | solution.py:107
  230.5 2.3 reshape.120
  232.9 1.9 convolution_convert_fusion
  234.8 0.5 multiply_convert_fusion.1
  235.3 0.6 convolution_convert_fusion.1
  235.9 0.6 convolution_convert_fusion.2
  236.4 2.1 pad_maximum_fusion
  238.5 6.3 copy.60
  244.8 1.3 copy-done.1
  246.1 0.6 fusion.23
  246.7 0.7 copy-done.4
  247.4 0.6 fusion
  248.0 1.3 reshape.121
  249.3 28.4 %all-to-all-start.3 = ((bf16[32,7,2560]{2,1,0:T(8,128)(2,1)}), bf16[32,7,2560]{2,1,0:T(8,128)(2,1)S(1)}, u32[]{:S(2)}, u32[]{:S(2)}) async-start(bf16[32,7,2560]{2,1,0:T(8,128)(2,1)} %reshape.121), calls=%async_computation.3 | async-start | bytes 2621440 | tf_op jit(solution)/shard_map/all_to_all | solution.py:32
  277.9 0.9 convolution_bitcast_fusion
  278.8 0.9 fusion.2
  279.8 56.8 %all-to-all-done.3 = bf16[32,7,2560]{2,1,0:T(8,128)(2,1)S(1)} async-done(((bf16[32,7,2560]{2,1,0:T(8,128)(2,1)}), bf16[32,7,2560]{2,1,0:T(8,128)(2,1)S(1)}, u32[]{:S(2)}, u32[]{:S(2)}) %all-to-all-start.3) | async-done | bytes 1146912 | tf_op jit(solution)/shard_map/all_to_all | solution.py:32
  336.5 0.3 bitcast_reduce_fusion
  336.8 0.3 convolution_bitcast_fusion.1
  337.1 0.8 fusion.3
  337.9 75.4 %reduce-scatter.4.cloned.1.call-done = bf16[160,768]{1,0:T(8,128)(2,1)} async-done(((bf16[2560,768]{1,0:T(8,128)(2,1)}), bf16[160,768]{1,0:T(8,128)(2,1)}) %reduce-scatter.4.cloned.1.call-update) | async-done | bytes 245776
  413.3 1.1 copy.61
  414.5 0.8 copy.47
  415.3 0.8 copy.48
  416.1 0.8 copy.49
  416.8 385.5 %all-reduce.2.cloned.1.call-done = f32[2560,8]{0,1:T(8,128)} async-done(((f32[2560,8]{0,1:T(8,128)}), f32[2560,8]{0,1:T(8,128)}) %all-reduce.2.cloned.1.call-update) | async-done | bytes 81936 | tf_op jit(solution)/shard_map/psum | solution.py:102
  802.4 1.5 copy.78
  (50 shorter events, 1.2 us)
Async XLA Ops:
  8.0 89.8 %copy-start = (bf16[2560,256]{1,0:T(8,128)(2,1)S(1)}, bf16[2560,256]{1,0:T(8,128)(2,1)}, u32[]{:S(2)}) copy-start(bf16[2560,256]{1,0:T(8,128)(2,1)} %param.12) | copy-start | bytes 3932164
  94.7 1.9 copy-start.3
  96.6 1.2 copy-start.8
  101.7 8.8 %copy-start.5 = (bf16[8,2560]{1,0:T(8,128)(2,1)S(1)}, bf16[8,2560]{1,0:T(8,128)(2,1)}, u32[]{:S(2)}) copy-start(bf16[8,2560]{1,0:T(8,128)(2,1)} %param.7) | copy-start | bytes 122884
  101.7 8.8 %copy-start.6 = (f32[2560,8]{0,1:T(8,128)S(1)}, f32[2560,8]{0,1:T(8,128)}, u32[]{:S(2)}) copy-start(f32[2560,8]{0,1:T(8,128)} %param.9) | copy-start | bytes 245764
  101.7 47.2 %all-to-all-start.1 = ((bf16[32,7,2560]{2,1,0:T(8,128)(2,1)}), bf16[32,7,2560]{2,1,0:T(8,128)(2,1)}, u32[]{:S(2)}, u32[]{:S(2)}) async-start(bf16[32,7,2560]{2,1,0:T(8,128)(2,1)} %reshape.116), calls=%async_computation.1 | async-start | bytes 2621440 | tf_op jit(solution)/shard_map/all_to_all | solution.py:81
  110.4 303.0 %reduce-scatter.4.cloned.1.call-start = ((), (), s32[]{:S(2)}) async-start(), calls=%async_computation.6 | async-start | bytes 4177920
  148.9 2.8 copy-start.12
  151.8 0.5 copy-start.13
  155.4 0.6 copy-start.10
  232.9 1.9 copy-start.2
  232.9 2.0 copy-start.9
  232.9 2.0 copy-start.15
  244.8 1.3 copy-start.1
  246.1 1.3 copy-start.4
  249.3 28.5 %copy-start.14 = (f32[8]{0:T(128)S(1)}, f32[8]{0:T(128)}, u32[]{:S(2)}) copy-start(f32[8]{0:T(128)} %copy-done.13) | copy-start | bytes 100
  249.3 29.5 %copy-start.11 = (f32[8,1,8,7]{2,1,3,0:T(1,128)S(1)}, f32[8,1,8,7]{2,1,3,0:T(1,128)}, u32[]{:S(2)}) copy-start(f32[8,1,8,7]{2,1,3,0:T(1,128)} %copy-done.10) | copy-start | bytes 5380
  249.3 87.2 %all-to-all-start.3 = ((bf16[32,7,2560]{2,1,0:T(8,128)(2,1)}), bf16[32,7,2560]{2,1,0:T(8,128)(2,1)S(1)}, u32[]{:S(2)}, u32[]{:S(2)}) async-start(bf16[32,7,2560]{2,1,0:T(8,128)(2,1)} %reshape.121), calls=%async_computation.3 | async-start | bytes 2621440 | tf_op jit(solution)/shard_map/all_to_all | solution.py:32
  277.7 524.7 %all-reduce.2.cloned.1.call-start = ((), (), s32[]{:S(2)}) async-start(), calls=%async_computation.5 | async-start | bytes 163840 | tf_op jit(solution)/shard_map/psum | solution.py:102
  277.9 59.2 %copy-start.7 = (f32[2560,8]{0,1:T(8,128)S(1)}, f32[2560,8]{0,1:T(8,128)}, u32[]{:S(2)}) copy-start(f32[2560,8]{0,1:T(8,128)} %param.9) | copy-start | bytes 245764
Sparse Core Ops, SparseCore 0:
  244.9 168.3 reduce-scatter.3
Sparse Core Ops, SparseCore 1:
  284.2 518.1 all-reduce.1
where the time goes:
time: 812 us; the launch traced here: 811 us
  waiting for transfers between devices  555 us (68%)
  blocking collectives  157 us (19%)
  starting transfers between devices  37.2 us (5%)
  local copies, waits for them, and re-layouts  24.5 us (3%)
  matrix products  16.2 us (2%)
  between operations  15.8 us (2%)
    psum x1, waiting for transfers between devices, local(): grad_router = lax.psum(router_part, ('dp', 'expert'))  386 us
    all_to_all x1, blocking collectives, local(): lax.all_to_all(outgoing_all, 'expert', split_axis=0, concat_axis=0, tiled...  82.5 us
    unnamed x3, waiting for transfers between devices  75.4 us
    all_to_all x1, blocking collectives, local(): lax.all_to_all(grad_outgoing_all, 'expert', split_axis=0, concat_axis=0,...  74.3 us
    all_to_all x1, waiting for transfers between devices, return_grads(): lax.all_to_all(input_part, 'expert', split_axis=0, concat_axis=0, tiled=T...  56.8 us
    all_to_all x1, waiting for transfers between devices, local(): lax.all_to_all(output, 'expert', split_axis=0, concat_axis=0, tiled=True)  36.9 us
    all_to_all x1, starting transfers between devices, return_grads(): lax.all_to_all(input_part, 'expert', split_axis=0, concat_axis=0, tiled=T...  28.4 us
  transfers between devices with their start and end apart: 4, of which 4 were waited for; matrix products, arithmetic and copies ran while one was open for 1% of the time, Pallas kernels for 0%

commit v1 on v0

--- a/solution.py
+++ b/solution.py
@@ -99,7 +99,8 @@
     logit_grad = (gate_pull - mean_pull) / denominator * affinity * (1.0 - affinity)
     per_logit = jnp.sum(choose_f * logit_grad[:, :, None], axis=1)
     router_part = jnp.dot(tokens_wide.T, per_logit, precision=highest)
-    grad_router = lax.psum(router_part, ("dp", "expert"))
+    blocks = lax.all_gather(router_part, ("dp", "expert"), axis=0, tiled=False)
+    grad_router = blocks.sum(axis=0)
     slot_gate = jnp.sum(gate_table, axis=0)
     grad_outgoing = (slot_gate[:, :, None] * grad_slots.astype(jnp.float32)).astype(jnp.bfloat16)
     grad_outgoing_all = jnp.repeat(grad_outgoing, sharing, axis=0)

time: 812 us -> 1240 us (1.53)
  waiting for transfers between devices: 555 us -> 964 us
  other arithmetic: 6.26 us -> 22.9 us
    all_gather x0 -> x1, waiting for transfers between devices: none -> 781 us  [local(): blocks = lax.all_gather(router_part, ('dp', 'expert'), axis=0, tiled=False)]
    psum x1 -> x0, waiting for transfers between devices: 386 us -> none  [local(): grad_router = lax.psum(router_part, ('dp', 'expert'))]
    reduce_sum x0 -> x1, other arithmetic: none -> 16.6 us  [local(): grad_router = blocks.sum(axis=0)]
where the time goes in v1:
time: 1240 us
  waiting for transfers between devices  964 us (78%)
  blocking collectives  157 us (13%)
  starting transfers between devices  38.5 us (3%)
  other arithmetic  22.9 us (2%)
  local copies, waits for them, and re-layouts  22.3 us (2%)
  matrix products  16.2 us (1%)
  between operations  15.8 us (1%)
    all_gather x1, waiting for transfers between devices, local(): blocks = lax.all_gather(router_part, ('dp', 'expert'), axis=0, tiled=False)  781 us
    all_to_all x1, blocking collectives, local(): lax.all_to_all(outgoing_all, 'expert', split_axis=0, concat_axis=0, tiled...  82.4 us
    unnamed x3, waiting for transfers between devices  78.5 us
    all_to_all x1, blocking collectives, local(): lax.all_to_all(grad_outgoing_all, 'expert', split_axis=0, concat_axis=0,...  74.7 us
    all_to_all x1, waiting for transfers between devices, return_grads(): lax.all_to_all(input_part, 'expert', split_axis=0, concat_axis=0, tiled=T...  68.9 us
    all_to_all x1, waiting for transfers between devices, local(): lax.all_to_all(output, 'expert', split_axis=0, concat_axis=0, tiled=True)  36.5 us
    all_to_all x1, starting transfers between devices, return_grads(): lax.all_to_all(input_part, 'expert', split_axis=0, concat_axis=0, tiled=T...  29.8 us
  transfers between devices with their start and end apart: 4, of which 4 were waited for; matrix products, arithmetic and copies ran while one was open for 1% of the time, Pallas kernels for 0%

profile of v1, /device:TPU:1, one launch (start us, length us, event | category | flops | bytes accessed | tf_op | source)
XLA Modules:
  0.0 1237.4 jit_solution(2930279962897470249)
XLA Ops:
  8.0 0.9 copy.37
  9.1 0.2 select_reduce_fusion.3
  9.5 1.0 convolution_convert_fusion.5
  10.7 82.4 %all_to_all.21 = bf16[32,7,2560]{2,1,0:T(8,128)(2,1)} all-to-all(bf16[32,7,2560]{2,1,0:T(8,128)(2,1)S(1)} %bitcast.60), channel_id=1, replica_groups=mesh['dp'=16,'expert'=32] {'expert'}, dimensions={0} | all-to-all | bytes 2293760 | tf_op jit(solution)/shard_map/all_to_all | solution.py:73
  93.1 1.5 reshape.115
  94.7 1.9 fusion.22
  96.6 1.2 multiply_convert_fusion.3
  97.7 1.6 convolution_convert_fusion.3
  99.3 2.3 reshape.116
  101.6 8.6 all-to-all-start.1
  110.3 0.8 fusion.21
  111.1 0.7 broadcast_multiply_fusion
  111.9 36.5 %all-to-all-done.1 = bf16[32,7,2560]{2,1,0:T(8,128)(2,1)} async-done(((bf16[32,7,2560]{2,1,0:T(8,128)(2,1)}), bf16[32,7,2560]{2,1,0:T(8,128)(2,1)}, u32[]{:S(2)}, u32[]{:S(2)}) %all-to-all-start.1) | async-done | bytes 1146912 | tf_op jit(solution)/shard_map/all_to_all | solution.py:81
  148.4 1.6 bitcast_reduce_fusion.1
  150.0 1.1 multiply_reduce_fusion
  151.1 0.2 select_reduce_fusion.1
  151.3 0.5 copy-done.14
  151.8 0.6 fusion.19
  152.4 1.4 copy.51
  153.8 1.0 fusion.6
  154.9 0.6 copy-done.11
  155.8 74.7 %all_to_all.22 = bf16[32,7,2560]{2,1,0:T(8,128)(2,1)} all-to-all(bf16[32,7,2560]{2,1,0:T(8,128)(2,1)S(1)} %bitcast.61), channel_id=1, replica_groups=mesh['dp'=16,'expert'=32] {'expert'}, dimensions={0} | all-to-all | bytes 2293760 | tf_op jit(solution)/shard_map/all_to_all | solution.py:108
  230.5 2.3 reshape.120
  232.8 1.9 convolution_convert_fusion
  234.8 0.5 multiply_convert_fusion.1
  235.3 0.6 convolution_convert_fusion.1
  235.8 0.6 convolution_convert_fusion.2
  236.4 2.1 pad_maximum_fusion
  238.5 6.3 copy.60
  244.8 0.6 copy-done.15
  245.6 0.9 convolution_bitcast_fusion
  246.5 0.6 fusion.23
  247.0 0.7 copy-done.5
  247.8 0.6 fusion
  248.4 1.3 reshape.121
  249.6 29.8 %all-to-all-start.3 = ((bf16[32,7,2560]{2,1,0:T(8,128)(2,1)}), bf16[32,7,2560]{2,1,0:T(8,128)(2,1)S(1)}, u32[]{:S(2)}, u32[]{:S(2)}) async-start(bf16[32,7,2560]{2,1,0:T(8,128)(2,1)} %reshape.121), calls=%async_computation.3 | async-start | bytes 2621440 | tf_op jit(solution)/shard_map/all_to_all | solution.py:32
  279.5 0.9 fusion.2
  280.4 68.9 %all-to-all-done.3 = bf16[32,7,2560]{2,1,0:T(8,128)(2,1)S(1)} async-done(((bf16[32,7,2560]{2,1,0:T(8,128)(2,1)}), bf16[32,7,2560]{2,1,0:T(8,128)(2,1)S(1)}, u32[]{:S(2)}, u32[]{:S(2)}) %all-to-all-start.3) | async-done | bytes 1146912 | tf_op jit(solution)/shard_map/all_to_all | solution.py:32
  349.3 0.3 bitcast_reduce_fusion
  349.6 0.3 convolution_bitcast_fusion.1
  349.9 0.8 fusion.3
  350.7 78.5 %reduce-scatter.4.cloned.1.call-done = bf16[160,768]{1,0:T(8,128)(2,1)} async-done(((bf16[2560,768]{1,0:T(8,128)(2,1)}), bf16[160,768]{1,0:T(8,128)(2,1)}) %reduce-scatter.4.cloned.1.call-update) | async-done | bytes 245776
  429.2 1.1 copy.61
  430.4 0.8 copy.47
  431.2 0.8 copy.48
  431.9 0.8 copy.49
  432.7 780.6 %all-gather.3.cloned.1.call-done = f32[1310720,8]{0,1:T(8,128)} async-done(((f32[2560,8]{0,1:T(8,128)}), f32[1310720,8]{0,1:T(8,128)}) %all-gather.3.cloned.1.call-update) | async-done | bytes 41943056 | tf_op jit(solution)/shard_map/all_gather | solution.py:102
  1213.3 16.6 %reduce_sum.129 = f32[2560,8]{0,1:T(8,128)} reduce(f32[512,2560,8]{1,2,0:T(8,128)} %bitcast.59, f32[]{:T(128)} %constant.16.clone.1), dimensions={0}, to_apply=%region_13.14 | reduce | flops 10465280 | bytes 42024964 | tf_op jit(solution)/shard_map/reduce_sum | solution.py:103
  (52 shorter events, 1.2 us)
Async XLA Ops:
  8.0 89.7 %copy-start = (bf16[2560,256]{1,0:T(8,128)(2,1)S(1)}, bf16[2560,256]{1,0:T(8,128)(2,1)}, u32[]{:S(2)}) copy-start(bf16[2560,256]{1,0:T(8,128)(2,1)} %param.12) | copy-start | bytes 3932164
  94.7 1.9 copy-start.4
  96.6 1.2 copy-start.9
  101.6 8.7 copy-start.6
  101.6 8.7 copy-start.7
  101.6 46.7 %all-to-all-start.1 = ((bf16[32,7,2560]{2,1,0:T(8,128)(2,1)}), bf16[32,7,2560]{2,1,0:T(8,128)(2,1)}, u32[]{:S(2)}, u32[]{:S(2)}) async-start(bf16[32,7,2560]{2,1,0:T(8,128)(2,1)} %reshape.116), calls=%async_computation.1 | async-start | bytes 2621440 | tf_op jit(solution)/shard_map/all_to_all | solution.py:81
  110.3 318.9 %reduce-scatter.4.cloned.1.call-start = ((), (), s32[]{:S(2)}) async-start(), calls=%async_computation.6 | async-start | bytes 4177920
  148.4 2.8 copy-start.13
  151.3 0.5 copy-start.14
  154.8 0.6 copy-start.11
  232.8 2.0 copy-start.3
  232.8 2.0 copy-start.10
  232.8 2.0 copy-start.16
  244.8 0.7 copy-start.15
  244.8 1.7 copy-start.2
  244.8 968.5 %all-gather.3.cloned.1.call-start = ((), (), s32[]{:S(2)}) async-start(), calls=%async_computation.5 | async-start | bytes 42024960 | tf_op jit(solution)/shard_map/all_gather | solution.py:102
  246.5 1.3 copy-start.5
  249.6 29.8 %copy-start.12 = (f32[8,1,8,7]{2,1,3,0:T(1,128)S(1)}, f32[8,1,8,7]{2,1,3,0:T(1,128)}, u32[]{:S(2)}) copy-start(f32[8,1,8,7]{2,1,3,0:T(1,128)} %copy-done.11) | copy-start | bytes 5380
  249.6 99.7 %all-to-all-start.3 = ((bf16[32,7,2560]{2,1,0:T(8,128)(2,1)}), bf16[32,7,2560]{2,1,0:T(8,128)(2,1)S(1)}, u32[]{:S(2)}, u32[]{:S(2)}) async-start(bf16[32,7,2560]{2,1,0:T(8,128)(2,1)} %reshape.121), calls=%async_computation.3 | async-start | bytes 2621440 | tf_op jit(solution)/shard_map/all_to_all | solution.py:32
  279.5 70.4 %copy-start.8 = (f32[2560,8]{0,1:T(8,128)S(1)}, f32[2560,8]{0,1:T(8,128)}, u32[]{:S(2)}) copy-start(f32[2560,8]{0,1:T(8,128)} %param.9) | copy-start | bytes 245764
  1213.3 16.6 %copy-start.1 = (bf16[2560,256]{1,0:T(8,128)(2,1)S(1)}, bf16[2560,256]{1,0:T(8,128)(2,1)}, u32[]{:S(2)}) copy-start(bf16[2560,256]{1,0:T(8,128)(2,1)} %param.12) | copy-start | bytes 3932164
Sparse Core Ops, SparseCore 0:
  244.9 184.2 reduce-scatter.3
Sparse Core Ops, SparseCore 1:
  248.1 965.2 all-gather.2
